TPU v7x, 128 devices: a whole 4x4x4 slice. The times are simulated.
128 devices in a mesh: dp: 16 (over y, x), head: 8 (over z, core).
Axes of the slice: x: 4, y: 4, z: 4, core: 2. Of those that a mesh axis runs over, the one named last changes fastest.
Arguments:
- slot_token_ids: int32 [128, 512], P('dp'), may hold values from 0 to 50264
- lengths: int32 [128], P('dp'), may hold values from 64 to 512, as said below
- labels: int32 [128], P('dp'), may hold values from 0 to 2
- optimizer_step_count: int32 [], replicated, may hold values from 2 to 20
- token_embedding_table: bfloat16 [50304, 1024], P('dp', 'head'), may hold values from -6 to 6
- positions: bfloat16 [512, 1024], replicated, may hold values from -4 to 4
- query_key_value_weight: bfloat16 [3, 1024, 1024], P(None, None, 'head'), may hold values from -0.1875 to 0.1875
- attention_output_weight: bfloat16 [1024, 1024], P('head'), may hold values from -0.8 to 0.8
- feedforward_input_weight: bfloat16 [1024, 4096], P(None, 'head'), may hold values from -0.1875 to 0.1875
- feedforward_output_weight: bfloat16 [4096, 1024], P('head'), may hold values from -0.09375 to 0.09375
- layer_norm_gains: float32 [3, 1024], replicated, may hold values from 0.5 to 1.5
- layer_norm_biases: float32 [3, 1024], replicated, may hold values from -2 to 2
- classifier: bfloat16 [3, 1024], replicated, may hold values from -0.75 to 0.75
- adapter_down_maps: float32 [2, 1024, 16], replicated, may hold values from -0.1875 to 0.1875
- adapter_up_maps: float32 [2, 16, 1024], P(None, None, 'head'), may hold values from -1.5 to 1.5
- down_first_moment: float32 [2, 1024, 16], P(None, 'dp'), may hold values from -0.0078125 to 0.0078125
- down_second_moment: float32 [2, 1024, 16], P(None, 'dp'), may hold values from 2.1972657e-08 to 9.1552735e-08
- up_first_moment: float32 [2, 16, 1024], P(None, None, ('head', 'dp')), may hold values from -0.0078125 to 0.0078125
- up_second_moment: float32 [2, 16, 1024], P(None, None, ('head', 'dp')), may hold values from 2.1972657e-08 to 9.1552735e-08
- down_privacy_noise: float32 [2, 1024, 16], P(None, 'dp'), may hold values from -6 to 6
- up_privacy_noise: float32 [2, 16, 1024], P(None, None, ('head', 'dp')), may hold values from -6 to 6
Outputs:
- loss: float32 [], replicated
- example_norms: float32 [128], P(('dp', 'head'))
- a_moment1: float32 [2, 1024, 16], P(None, 'dp')
- a_moment2: float32 [2, 1024, 16], P(None, 'dp')
- a_weight: float32 [2, 1024, 16], P(None, 'dp')
- b_moment1: float32 [2, 16, 1024], P(None, None, ('head', 'dp'))
- b_moment2: float32 [2, 16, 1024], P(None, None, ('head', 'dp'))
- b_weight: float32 [2, 16, 1024], P(None, None, ('head', 'dp'))
- lamb_norms: float32 [4, 2], replicated
Inputs may be any that keep to these rules, and one draw needn't show every extreme that they name: `lengths`: valid tokens of each example; some example has exactly 512.
All inputs are finite; a program needn't handle non-finite values.
Results may differ from a plain program's by a relative error of at most 0.0059.
Values may be sent and summed in bfloat16 or wider, within the bound.
No kernel may reach another device: no remote copies, remote signals or barrier semaphores. Data moves between devices by JAX's collectives and lax.ppermute only.
A program may use at most 256 MiB of HBM per device.

v0:
```python
import jax
import jax.numpy as jnp
from jax import lax
from jax.sharding import PartitionSpec as P

HDIM = 64
MICRO = 4
precise = lax.Precision.HIGHEST
adapter_scale = 2.0
clip_bound = 1.0
noise_mult = 0.6
smooth_rate = 0.1
beta_one = 0.9
beta_two = 0.999
adam_eps = 1e-06
decay_rate = 0.01
learn_rate = 0.25
norm_eps = 1e-05
contract_last = (((1,), (1,)), ((), ()))


def gelu_exact(inputs):
    return jax.nn.gelu(inputs, approximate=False)


def norm_rows(inputs, gain, bias):
    centre = inputs - jnp.mean(inputs, -1, keepdims=True)
    inv_std = lax.rsqrt(jnp.mean(centre * centre, -1, keepdims=True) + norm_eps)
    return (centre * inv_std * gain + bias, inv_std)


def norm_back(grad, normed, inv_std, gain, bias):
    x_hat = (normed - bias) / gain
    scaled = grad * gain
    return inv_std * (
        scaled
        - jnp.mean(scaled, -1, keepdims=True)
        - x_hat * jnp.mean(scaled * x_hat, -1, keepdims=True)
    )


def branch_add(partial_out, resid, gain, bias):
    total = lax.psum(partial_out, "head")
    return norm_rows(resid + total, gain, bias)


def masked_scores(query_h, key_h, valid_mask):
    scores = jnp.einsum(
        "eqhd,ekhd->ehqk", query_h, key_h, preferred_element_type=jnp.float32
    ) * HDIM ** (-0.5)
    return jnp.where(valid_mask[:, None, None, :], scores, -1e30)


def layer_forward(
    hidden_initial, valid_mask, length_float, class_label, frozen_params, adapter_reduced
):
    w_qkv, w_o, w_in, w_out, gains, biases, class_w = frozen_params
    down_pair, up_reduced = adapter_reduced
    example_count, sequence_length = valid_mask.shape
    width = hidden_initial.shape[1]
    local_w = w_o.shape[0]
    adapter_width = up_reduced.shape[1]
    shape4 = (example_count, sequence_length, local_w // HDIM, HDIM)
    hidden_reduced = hidden_initial.astype(jnp.bfloat16)
    adapter_activation = jnp.dot(
        hidden_reduced, down_pair, preferred_element_type=jnp.float32
    ).astype(jnp.bfloat16)
    query_low = (
        (
            jnp.dot(hidden_reduced, w_qkv[0], preferred_element_type=jnp.float32)
            + adapter_scale
            * jnp.dot(
                adapter_activation[:, :adapter_width],
                up_reduced[0],
                preferred_element_type=jnp.float32,
            )
        )
        .astype(jnp.bfloat16)
        .reshape(shape4)
    )
    key_low = (
        jnp.dot(hidden_reduced, w_qkv[1], preferred_element_type=jnp.float32)
        .astype(jnp.bfloat16)
        .reshape(shape4)
    )
    value_low = (
        (
            jnp.dot(hidden_reduced, w_qkv[2], preferred_element_type=jnp.float32)
            + adapter_scale
            * jnp.dot(
                adapter_activation[:, adapter_width:],
                up_reduced[1],
                preferred_element_type=jnp.float32,
            )
        )
        .astype(jnp.bfloat16)
        .reshape(shape4)
    )
    scores = masked_scores(query_low, key_low, valid_mask)
    row_top = jnp.max(scores, -1, keepdims=True)
    log_total = row_top + jnp.log(jnp.sum(jnp.exp(scores - row_top), -1, keepdims=True))
    attn_prob = jnp.exp(scores - log_total)
    context = (
        jnp.einsum(
            "ehqk,ekhd->eqhd",
            attn_prob.astype(jnp.bfloat16),
            value_low,
            preferred_element_type=jnp.float32,
        )
        .astype(jnp.bfloat16)
        .reshape(-1, local_w)
    )
    hidden_one, std_one = branch_add(
        jnp.dot(context, w_o, preferred_element_type=jnp.float32),
        hidden_initial,
        gains[1],
        biases[1],
    )
    ffn_pre = jnp.dot(hidden_one.astype(jnp.bfloat16), w_in, preferred_element_type=jnp.float32)
    ffn_part = jnp.dot(
        gelu_exact(ffn_pre).astype(jnp.bfloat16), w_out, preferred_element_type=jnp.float32
    )
    hidden_two, std_two = branch_add(ffn_part, hidden_one, gains[2], biases[2])
    valid_f = valid_mask.astype(jnp.float32)
    pooled = (
        jnp.sum(hidden_two.reshape(example_count, sequence_length, width) * valid_f[..., None], 1)
        / length_float[:, None]
    )
    logits = lax.dot_general(
        pooled.astype(jnp.bfloat16), class_w, contract_last, preferred_element_type=jnp.float32
    )
    log_prob = jax.nn.log_softmax(logits, -1)
    target = (1.0 - smooth_rate) * jax.nn.one_hot(
        class_label, class_w.shape[0], dtype=jnp.float32
    ) + smooth_rate / class_w.shape[0]
    losses = -jnp.sum(target * log_prob, -1)
    d_logit = jnp.exp(log_prob) - target
    d_pooled = jnp.dot(d_logit, class_w.astype(jnp.float32), precision=precise)
    d_two = (d_pooled[:, None, :] * (valid_f / length_float[:, None])[..., None]).reshape(-1, width)
    d_sum_two = norm_back(d_two, hidden_two, std_two, gains[2], biases[2])
    grad_act = lax.dot_general(
        d_sum_two.astype(jnp.bfloat16), w_out, contract_last, preferred_element_type=jnp.float32
    )
    d_pre = jax.vjp(gelu_exact, ffn_pre)[1](grad_act)[0].astype(jnp.bfloat16)
    back_part = lax.dot_general(d_pre, w_in, contract_last, preferred_element_type=jnp.float32)
    d_one = d_sum_two + lax.psum(back_part, "head")
    d_attn = norm_back(d_one, hidden_one, std_one, gains[1], biases[1]).astype(jnp.bfloat16)
    d_context = (
        lax.dot_general(d_attn, w_o, contract_last, preferred_element_type=jnp.float32)
        .astype(jnp.bfloat16)
        .reshape(shape4)
    )
    attn_prob = jnp.exp(masked_scores(query_low, key_low, valid_mask) - log_total)
    d_value = jnp.einsum(
        "ehqk,eqhd->ekhd",
        attn_prob.astype(jnp.bfloat16),
        d_context,
        preferred_element_type=jnp.float32,
    ).astype(jnp.bfloat16)
    d_prob = jnp.einsum("eqhd,ekhd->ehqk", d_context, value_low, preferred_element_type=jnp.float32)
    d_score = (attn_prob * (d_prob - jnp.sum(attn_prob * d_prob, -1, keepdims=True))).astype(
        jnp.bfloat16
    )
    d_query = (
        jnp.einsum("ehqk,ekhd->eqhd", d_score, key_low, preferred_element_type=jnp.float32)
        * HDIM ** (-0.5)
    ).astype(jnp.bfloat16)
    dq_rows = d_query.reshape(-1, local_w)
    dv_rows = d_value.reshape(-1, local_w)
    example_activation = adapter_activation.reshape(
        example_count, sequence_length, 2 * adapter_width
    )
    up_gradient = adapter_scale * jnp.stack(
        [
            jnp.einsum(
                "elr,eld->erd",
                example_activation[..., :adapter_width],
                dq_rows.reshape(example_count, sequence_length, local_w),
                preferred_element_type=jnp.float32,
            ),
            jnp.einsum(
                "elr,eld->erd",
                example_activation[..., adapter_width:],
                dv_rows.reshape(example_count, sequence_length, local_w),
                preferred_element_type=jnp.float32,
            ),
        ],
        1,
    )
    inner_portion = adapter_scale * jnp.concatenate(
        [
            lax.dot_general(
                dq_rows, up_reduced[0], contract_last, preferred_element_type=jnp.float32
            ),
            lax.dot_general(
                dv_rows, up_reduced[1], contract_last, preferred_element_type=jnp.float32
            ),
        ],
        1,
    )
    inner_full = lax.psum(inner_portion, "head")
    inner_sum = inner_full.astype(jnp.bfloat16)
    grad_both = jnp.einsum(
        "eld,elr->edr",
        hidden_reduced.reshape(example_count, sequence_length, width),
        inner_sum.reshape(example_count, sequence_length, 2 * adapter_width),
        preferred_element_type=jnp.float32,
    )
    down_gradient = jnp.stack([grad_both[..., :adapter_width], grad_both[..., adapter_width:]], 1)
    return (losses, down_gradient, up_gradient)


def apply_blocks(hidden_rows, lengths, labels, frozen_params, adapter_reduced, encoder_block):
    example_count, sequence_length, width = hidden_rows.shape
    valid_all = jnp.arange(sequence_length)[None, :] < lengths[:, None]
    loss_list, down_list, up_list = ([], [], [])
    for block_idx in range(example_count // encoder_block):
        first_ex = block_idx * encoder_block
        last_ex = first_ex + encoder_block
        losses, down_gradient, up_gradient = layer_forward(
            hidden_rows[first_ex:last_ex].reshape(-1, width),
            valid_all[first_ex:last_ex],
            lengths[first_ex:last_ex].astype(jnp.float32),
            labels[first_ex:last_ex],
            frozen_params,
            adapter_reduced,
        )
        loss_list.append(losses)
        down_list.append(down_gradient)
        up_list.append(up_gradient)
    return (
        jnp.concatenate(loss_list, 0),
        jnp.concatenate(down_list, 0),
        jnp.concatenate(up_list, 0),
    )


def lamb_direction(weight, grad, first, second, step_number):
    first_new = beta_one * first + (1.0 - beta_one) * grad
    second_new = beta_two * second + (1.0 - beta_two) * grad * grad
    direction = (
        first_new
        / (1.0 - jnp.power(beta_one, step_number))
        / (jnp.sqrt(second_new / (1.0 - jnp.power(beta_two, step_number))) + adam_eps)
        + decay_rate * weight
    )
    return (first_new, second_new, direction)


def per_device(
    slot_token_ids,
    lengths,
    labels,
    optimizer_step_count,
    token_embedding_table,
    positions,
    query_key_value_weight,
    attention_output_weight,
    feedforward_input_weight,
    feedforward_output_weight,
    layer_norm_gains,
    layer_norm_biases,
    classifier,
    adapter_down_maps,
    adapter_up_maps,
    down_first_moment,
    down_second_moment,
    up_first_moment,
    up_second_moment,
    down_privacy_noise,
    up_privacy_noise,
):
    n_head = lax.axis_size("head")
    dataset_size = lax.axis_size("dp")
    ex_dev, sequence_length = slot_token_ids.shape
    width = positions.shape[1]
    every_ids = lax.all_gather(slot_token_ids, "dp", axis=0, tiled=True).reshape(-1)
    vocab_local = token_embedding_table.shape[0]
    offset = lax.axis_index("dp") * vocab_local
    ids_here = every_ids - offset
    inside = (ids_here >= 0) & (ids_here < vocab_local)
    picked = jnp.take(token_embedding_table, jnp.clip(ids_here, 0, vocab_local - 1), axis=0)
    columns = lax.psum_scatter(
        jnp.where(inside[:, None], picked.astype(jnp.float32), 0.0).astype(jnp.bfloat16),
        "dp",
        scatter_dimension=0,
        tiled=True,
    )
    pos_f = positions.astype(jnp.float32)[None]
    down_reduced = adapter_down_maps.astype(jnp.bfloat16)
    down_pair = jnp.concatenate([down_reduced[0], down_reduced[1]], 1)
    micro_examples = ex_dev // MICRO
    own_share = ex_dev // n_head
    tokens = lax.all_gather(columns, "head", axis=1, tiled=True)
    hidden_all, unused_std = norm_rows(
        tokens.astype(jnp.float32).reshape(ex_dev, sequence_length, width) + pos_f,
        layer_norm_gains[0],
        layer_norm_biases[0],
    )
    frozen_params = (
        query_key_value_weight,
        attention_output_weight,
        feedforward_input_weight,
        feedforward_output_weight,
        layer_norm_gains,
        layer_norm_biases,
        classifier,
    )
    losses, grads_down, grads_up = apply_blocks(
        hidden_all,
        lengths,
        labels,
        frozen_params,
        (down_pair, adapter_up_maps.astype(jnp.bfloat16)),
        micro_examples,
    )
    part_sums = jnp.sum(grads_down * grads_down, (1, 2, 3)) / n_head + jnp.sum(
        grads_up * grads_up, (1, 2, 3)
    )
    arrived = lax.all_to_all(
        part_sums.reshape(n_head, own_share), "head", split_axis=0, concat_axis=0, tiled=True
    )
    example_norms = jnp.sqrt(jnp.sum(arrived, 0))
    own_factor = clip_bound / jnp.maximum(example_norms, clip_bound)
    factors = lax.all_gather(own_factor, "head", axis=0, tiled=True)
    sum_down = jnp.einsum("e,eabc->abc", factors, grads_down, precision=precise)
    sum_up = jnp.einsum("e,eabc->abc", factors, grads_up, precision=precise)
    loss_part = jnp.sum(losses) / n_head
    red_down, red_up = (
        lax.psum_scatter(sum_down, "dp", scatter_dimension=1, tiled=True),
        lax.psum_scatter(sum_up, "dp", scatter_dimension=2, tiled=True),
    )
    examples = ex_dev * dataset_size
    down_gradient = (red_down + noise_mult * clip_bound * down_privacy_noise) / examples
    up_gradient = (red_up + noise_mult * clip_bound * up_privacy_noise) / examples
    step_number = optimizer_step_count.astype(jnp.float32)
    down_rows = adapter_down_maps.shape[1] // dataset_size
    down_weight = lax.dynamic_slice_in_dim(
        adapter_down_maps, lax.axis_index("dp") * down_rows, down_rows, 1
    )
    up_columns = adapter_up_maps.shape[2] // dataset_size
    up_weight = lax.dynamic_slice_in_dim(
        adapter_up_maps, lax.axis_index("dp") * up_columns, up_columns, 2
    )
    down_momentum, down_velocity, dir_down = lamb_direction(
        down_weight, down_gradient, down_first_moment, down_second_moment, step_number
    )
    up_momentum, up_velocity, dir_up = lamb_direction(
        up_weight, up_gradient, up_first_moment, up_second_moment, step_number
    )
    sq_down = (
        jnp.stack(
            [jnp.sum(down_weight * down_weight, (1, 2)), jnp.sum(dir_down * dir_down, (1, 2))], 1
        )
        / n_head
    )
    sq_up = jnp.stack([jnp.sum(up_weight * up_weight, (1, 2)), jnp.sum(dir_up * dir_up, (1, 2))], 1)
    total_down, total_up, loss_sum = lax.psum((sq_down, sq_up, loss_part), ("dp", "head"))
    norm_table = jnp.sqrt(jnp.concatenate([total_down, total_up], 0))
    updated_down = (
        down_weight - learn_rate * (norm_table[:2, 0] / norm_table[:2, 1])[:, None, None] * dir_down
    )
    updated_up = (
        up_weight - learn_rate * (norm_table[2:, 0] / norm_table[2:, 1])[:, None, None] * dir_up
    )
    return (
        loss_sum / examples,
        example_norms,
        down_momentum,
        down_velocity,
        updated_down,
        up_momentum,
        up_velocity,
        updated_up,
        norm_table,
    )


def solution(mesh):
    placed = (
        P("dp", None),
        P("dp"),
        P("dp"),
        P(),
        P("dp", "head"),
        P(),
        P(None, None, "head"),
        P("head", None),
        P(None, "head"),
        P("head", None),
        P(),
        P(),
        P(),
        P(),
        P(None, None, "head"),
        P(None, "dp", None),
        P(None, "dp", None),
        P(None, None, ("head", "dp")),
        P(None, None, ("head", "dp")),
        P(None, "dp", None),
        P(None, None, ("head", "dp")),
    )
    return jax.shard_map(
        per_device,
        mesh=mesh,
        in_specs=placed,
        out_specs=(
            P(),
            P(("dp", "head")),
            P(None, "dp", None),
            P(None, "dp", None),
            P(None, "dp", None),
            P(None, None, ("head", "dp")),
            P(None, None, ("head", "dp")),
            P(None, None, ("head", "dp")),
            P(),
        ),
        check_vma=False,
    )
```

profile of v0, /device:TPU:1, one launch (start us, length us, event | category | flops | bytes accessed | tf_op | source)
XLA Modules:
  0.0 1647.0 jit_solution(5846328891770936799)
XLA Ops:
  7.3 19.8 %all_gather.9 = s32[128,512]{1,0:T(8,128)S(1)} all-gather(s32[8,512]{1,0:T(8,128)} %param.22), channel_id=1, replica_groups=mesh['dp'=16,'head'=8] {'dp'}, dimensions={0}, use_global_device_ids=true | all-gather | bytes 278528 | tf_op jit(solution)/shard_map/all_gather | solution.py:277
  28.1 229.0 %gather_fusion = bf16[65536,128]{1,0:T(8,128)(2,1)} fusion(bf16[3144,128]{1,0:T(8,128)(2,1)S(1)} %copy-done.1, s32[65536]{0:T(1024)S(1)} %broadcast_clamp_fusion), kind=kCustom, calls=%fused_computation | custom fusion | bytes 33816576 | tf_op jit(solution)/shard_map/jit(_take)/gather | solution.py:282
  257.0 46.3 %select_convert_fusion = bf16[65536,128]{1,0:T(8,128)(2,1)} fusion(bf16[65536,128]{1,0:T(8,128)(2,1)} %gather_fusion, pred[65536]{0:T(1024)(128)(4,1)S(1)} %compare_and_fusion, pred[65536]{0:T(1024)(128)(4,1)S(1)} %bitcast.555), kind=kLoop, calls=%fused_computation.1 | loop fusion | flops 33554432 | bytes 33685504 | tf_op jit(solution)/shard_map/convert_element_type | solution.py:284
  303.4 115.6 %reduce-scatter.6.cloned.1.call-done = bf16[4096,128]{1,0:T(8,128)(2,1)} async-done(((bf16[65536,128]{1,0:T(8,128)(2,1)}), bf16[4096,128]{1,0:T(8,128)(2,1)}) %reduce-scatter.6.cloned.1.call-update) | async-done | bytes 1048592 | tf_op jit(solution)/shard_map/reduce_scatter | solution.py:283
  423.8 51.6 %all-gather.2.cloned.1.call-done = bf16[4096,1024]{1,0:T(8,128)(2,1)} async-done(((bf16[4096,128]{1,0:T(8,128)(2,1)}), bf16[4096,1024]{1,0:T(8,128)(2,1)}) %all-gather.2.cloned.1.call-update) | async-done | bytes 8388624 | tf_op jit(solution)/shard_map/all_gather | solution.py:294
  475.4 5.1 fusion
  480.5 5.9 multiply_reduce_fusion
  486.4 6.1 multiply_add_fusion
  492.5 3.6 fusion.384
  496.1 4.8 fusion.383
  501.0 3.9 fusion.183
  565.9 3.3 fusion.135
  574.0 3.3 fusion.133
  580.3 183.9 %all-reduce.15.cloned.1.call-done = (f32[1024,1024]{1,0:T(8,128)}, f32[1024,1024]{1,0:T(8,128)}, f32[1024,1024]{1,0:T(8,128)}, f32[1024,1024]{1,0:T(8,128)}) async-done(((f32[1024,1024]{1,0:T(8,128)}, f32[1024,1024]{1,0:T(8,128)}, f32[1024,1024]{1,0:T(8,128)}, f32[1024,1024]{1,0:T(8,128)}), (f32[1024,1024]{1,0:T(8,128)}, f32[1024,1024]{1,0:T(8,128)}, f32[1024,1024]{1,0:T(8,128)}, ...) | async-done | bytes 16777232 | tf_op jit(solution)/shard_map/psum | solution.py:43
  764.3 4.1 fusion.382
  769.0 3.2 copy-done.31
  777.6 6.8 fusion.140
  784.4 6.7 fusion.138
  794.9 6.7 fusion.139
  806.8 6.7 fusion.137
  814.4 183.4 %all-reduce.13.cloned.1.call-done = (f32[1024,1024]{1,0:T(8,128)}, f32[1024,1024]{1,0:T(8,128)}, f32[1024,1024]{1,0:T(8,128)}, f32[1024,1024]{1,0:T(8,128)}) async-done(((f32[1024,1024]{1,0:T(8,128)}, f32[1024,1024]{1,0:T(8,128)}, f32[1024,1024]{1,0:T(8,128)}, f32[1024,1024]{1,0:T(8,128)}), (f32[1024,1024]{1,0:T(8,128)}, f32[1024,1024]{1,0:T(8,128)}, f32[1024,1024]{1,0:T(8,128)}, ...) | async-done | bytes 16777232 | tf_op jit(solution)/shard_map/psum | solution.py:43
  997.8 12.3 fusion.371
  1012.7 4.3 multiply_reduce_fusion.13
  1019.7 5.7 fusion.24
  1027.7 8.9 fusion.18
  1036.7 10.9 fusion.144
  1047.5 3.9 fusion.31
  1051.4 11.0 fusion.143
  1062.5 7.4 fusion.29
  1069.8 10.8 fusion.142
  1080.6 10.9 fusion.141
  1102.5 173.5 %all-reduce.11.cloned.1.call-done = (f32[1024,1024]{1,0:T(8,128)}, f32[1024,1024]{1,0:T(8,128)}, f32[1024,1024]{1,0:T(8,128)}, f32[1024,1024]{1,0:T(8,128)}) async-done(((f32[1024,1024]{1,0:T(8,128)}, f32[1024,1024]{1,0:T(8,128)}, f32[1024,1024]{1,0:T(8,128)}, f32[1024,1024]{1,0:T(8,128)}), (f32[1024,1024]{1,0:T(8,128)}, f32[1024,1024]{1,0:T(8,128)}, f32[1024,1024]{1,0:T(8,128)}, ...) | async-done | bytes 16777232 | tf_op jit(solution)/shard_map/psum | solution.py:146
  1276.0 7.9 fusion.370
  1286.7 3.5 convolution_convert_fusion
  1295.3 5.9 fusion.369
  1304.0 3.5 convolution_convert_fusion.1
  1307.6 3.5 multiply_reduce_fusion.4
  1312.6 5.9 fusion.368
  1321.4 3.5 convolution_convert_fusion.2
  1324.9 3.6 multiply_reduce_fusion.7
  1330.0 5.9 fusion.367
  1338.7 3.5 convolution_convert_fusion.3
  1359.7 29.7 %all-reduce.16 = (bf16[1024,32]{0,1:T(8,128)(2,1)}, bf16[1024,32]{0,1:T(8,128)(2,1)}, bf16[1024,32]{0,1:T(8,128)(2,1)}, bf16[1024,32]{0,1:T(8,128)(2,1)}) all-reduce(f32[1024,32]{0,1:T(8,128)S(1)} %maximum_multiply_fusion.3, f32[1024,32]{0,1:T(8,128)} %maximum_multiply_fusion.2, ...), channel_id=1, replica_groups=mesh['dp'=16,'head'=8] {'head'}, use_global_device_ids=true, to_apply=%region_73.75 | all-reduce | flops 131072 | bytes 786432 | tf_op jit(solution)/shard_map/psum | solution.py:201
  1396.8 10.8 all_to_all.6
  1409.6 12.5 all-reduce
  1426.7 64.2 %reduce-scatter.8.cloned.1.call-done = f32[2,16,8]{1,2,0:T(8,128)} async-done(((f32[2,16,128]{1,2,0:T(8,128)}), f32[2,16,8]{1,2,0:T(8,128)}) %reduce-scatter.8.cloned.1.call-update) | async-done | bytes 1040 | tf_op jit(solution)/shard_map/reduce_scatter | solution.py:331
  1492.3 74.0 %reduce-scatter.10.cloned.1.call-done = f32[64,32]{1,0:T(8,128)} async-done(((f32[1024,32]{1,0:T(8,128)}), f32[64,32]{1,0:T(8,128)}) %reduce-scatter.10.cloned.1.call-update) | async-done | bytes 8208
  1568.7 66.1 %all-reduce.1 = (f32[]{:T(128)}, f32[2,2]{0,1:T(2,128)S(1)}, f32[2,2]{0,1:T(2,128)S(1)}) all-reduce(f32[]{:T(128)S(6)} %div.320, f32[2,2]{0,1:T(2,128)S(1)} %pad_maximum_fusion.2, f32[2,2]{0,1:T(2,128)S(1)} %maximum_multiply_fusion.8), channel_id=1, replica_groups=mesh['dp'=16,'head'=8] {'dp','head'}, use_global_device_ids=true, to_apply=%region_45.47 | all-reduce | flops 9 | bytes 72 | tf_op jit(solution)/shard_map/psum | solution.py:358
  (611 shorter events, 159.5 us)
Async XLA Ops:
  7.2 770.4 %copy-start = (bf16[512,1024]{1,0:T(8,128)(2,1)S(1)}, bf16[512,1024]{1,0:T(8,128)(2,1)}, u32[]{:S(2)}) copy-start(bf16[512,1024]{1,0:T(8,128)(2,1)} %param.31) | copy-start | bytes 3145732
  7.2 20.9 %copy-start.1 = (bf16[3144,128]{1,0:T(8,128)(2,1)S(1)}, bf16[3144,128]{1,0:T(8,128)(2,1)}, u32[]{:S(2)}) copy-start(bf16[3144,128]{1,0:T(8,128)(2,1)} %param.26) | copy-start | bytes 2414596
  7.2 411.8 %reduce-scatter.6.cloned.1.call-start = ((), (), s32[]{:S(2)}) async-start(), calls=%async_computation.4 | async-start | bytes 17825792 | tf_op jit(solution)/shard_map/reduce_scatter | solution.py:283
  303.3 172.0 %all-gather.2.cloned.1.call-start = ((), (), s32[]{:S(2)}) async-start(), calls=%async_computation.5 | async-start | bytes 9437184 | tf_op jit(solution)/shard_map/all_gather | solution.py:294
  419.0 345.2 %all-reduce.15.cloned.1.call-start = ((), (), s32[]{:S(2)}) async-start(), calls=%async_computation.10 | async-start | bytes 33554432 | tf_op jit(solution)/shard_map/psum | solution.py:43
  420.7 151.7 %copy-start.88 = (bf16[2,16,128]{2,1,0:T(8,128)(2,1)}, bf16[2,16,128]{2,1,0:T(8,128)(2,1)S(1)}, u32[]{:S(2)}) copy-start(bf16[2,16,128]{2,1,0:T(8,128)(2,1)S(1)} %convert_element_type.351) | copy-start | bytes 24580
  422.0 151.4 %copy-start.111 = (pred[2,512]{1,0:T(4,128)(4,1)}, pred[2,512]{1,0:T(4,128)(4,1)S(1)}, u32[]{:S(2)}) copy-start(pred[2,512]{1,0:T(4,128)(4,1)S(1)} %get-tuple-element.137) | copy-start | bytes 3076
  500.9 19.8 %copy-start.32 = (f32[2,512,1024]{2,1,0:T(8,128)}, f32[2,512,1024]{2,1,0:T(8,128)S(1)}, u32[]{:S(2)}) copy-start(f32[2,512,1024]{2,1,0:T(8,128)S(1)} %get-tuple-element.79) | copy-start | bytes 12582916
  523.1 14.8 copy-start.71
  524.8 8.6 copy-start.53
  527.2 7.3 copy-start.49
  542.7 15.3 copy-start.69
  544.4 9.1 copy-start.55
  547.3 7.3 copy-start.51
  580.3 417.5 %all-reduce.13.cloned.1.call-start = ((), (), s32[]{:S(2)}) async-start(), calls=%async_computation.9 | async-start | bytes 33554432 | tf_op jit(solution)/shard_map/psum | solution.py:43
  764.3 4.7 copy-start.48
  768.4 5.0 copy-start.26
  777.5 6.8 copy-start.160
  784.4 6.7 copy-start.29
  784.4 6.7 copy-start.47
  794.9 6.7 copy-start.163
  794.9 6.7 copy-start.28
  794.9 6.7 copy-start.46
  813.5 462.4 %all-reduce.11.cloned.1.call-start = ((), (), s32[]{:S(2)}) async-start(), calls=%async_computation.8 | async-start | bytes 33554432 | tf_op jit(solution)/shard_map/psum | solution.py:146
  1010.1 9.6 copy-start.2
  1010.1 9.6 copy-start.6
  1010.1 17.6 %copy-start.4 = (f32[1024,1024]{1,0:T(8,128)}, f32[1024,1024]{1,0:T(8,128)S(1)}, u32[]{:S(2)}) copy-start(f32[1024,1024]{1,0:T(8,128)S(1)} %get-tuple-element.121) | copy-start | bytes 12582916
  1010.1 17.6 %copy-start.8 = (f32[1024,1024]{1,0:T(8,128)}, f32[1024,1024]{1,0:T(8,128)S(1)}, u32[]{:S(2)}) copy-start(f32[1024,1024]{1,0:T(8,128)S(1)} %get-tuple-element.125) | copy-start | bytes 12582916
  1012.7 4.3 copy-start.158
  1091.6 399.3 %reduce-scatter.8.cloned.1.call-start = ((), (), s32[]{:S(2)}) async-start(), calls=%async_computation.6 | async-start | bytes 139264 | tf_op jit(solution)/shard_map/reduce_scatter | solution.py:331
  1275.9 7.9 copy-start.27
  1276.0 7.9 copy-start.45
  1290.2 53.7 %copy-start.78 = (bf16[2,2,64,512]{3,2,1,0:T(8,128)(2,1)}, bf16[2,2,64,512]{3,2,1,0:T(8,128)(2,1)S(1)}, u32[]{:S(2)}) copy-start(bf16[2,2,64,512]{3,2,1,0:T(8,128)(2,1)S(1)} %convolution_convert_fusion) | copy-start | bytes 786436
  1290.2 5.0 copy-start.25
  1307.6 40.5 %copy-start.80 = (bf16[2,2,64,512]{3,2,1,0:T(8,128)(2,1)}, bf16[2,2,64,512]{3,2,1,0:T(8,128)(2,1)S(1)}, u32[]{:S(2)}) copy-start(bf16[2,2,64,512]{3,2,1,0:T(8,128)(2,1)S(1)} %convolution_convert_fusion.1) | copy-start | bytes 786436
  1307.6 5.1 copy-start.23
  1324.9 27.4 %copy-start.82 = (bf16[2,2,64,512]{3,2,1,0:T(8,128)(2,1)}, bf16[2,2,64,512]{3,2,1,0:T(8,128)(2,1)S(1)}, u32[]{:S(2)}) copy-start(bf16[2,2,64,512]{3,2,1,0:T(8,128)(2,1)S(1)} %convolution_convert_fusion.2) | copy-start | bytes 786436
  1324.9 5.1 copy-start.21
  1342.2 13.8 copy-start.84
  1358.9 32.7 %copy-start.38 = (bf16[2,512,1024]{2,1,0:T(8,128)(2,1)S(1)}, bf16[2,512,1024]{2,1,0:T(8,128)(2,1)}, u32[]{:S(2)}) copy-start(bf16[2,512,1024]{2,1,0:T(8,128)(2,1)} %get-tuple-element.84) | copy-start | bytes 6291460
  1423.1 143.2 %reduce-scatter.10.cloned.1.call-start = ((), (), s32[]{:S(2)}) async-start(), calls=%async_computation.7 | async-start | bytes 557056
  1423.2 67.7 %copy-start.122 = (f32[2,16,8]{1,2,0:T(8,128)S(1)}, f32[2,16,8]{1,2,0:T(8,128)}, u32[]{:S(2)}) copy-start(f32[2,16,8]{1,2,0:T(8,128)} %copy.338) | copy-start | bytes 3076
  1423.2 67.7 %copy-start.153 = (f32[2,16,8]{1,2,0:T(8,128)S(1)}, f32[2,16,8]{1,2,0:T(8,128)}, u32[]{:S(2)}) copy-start(f32[2,16,8]{1,2,0:T(8,128)} %param.42) | copy-start | bytes 3076
  1423.2 67.7 %copy-start.154 = (f32[2,16,8]{1,2,0:T(8,128)S(1)}, f32[2,16,8]{1,2,0:T(8,128)}, u32[]{:S(2)}) copy-start(f32[2,16,8]{1,2,0:T(8,128)} %param.40) | copy-start | bytes 3076
  1423.2 67.7 %copy-start.155 = (f32[2,16,8]{1,2,0:T(8,128)S(1)}, f32[2,16,8]{1,2,0:T(8,128)}, u32[]{:S(2)}) copy-start(f32[2,16,8]{1,2,0:T(8,128)} %param.39) | copy-start | bytes 3076
  1424.7 142.5 %copy-start.145 = (f32[2,64,16]{1,2,0:T(8,128)S(1)}, f32[2,64,16]{1,2,0:T(8,128)}, u32[]{:S(2)}) copy-start(f32[2,64,16]{1,2,0:T(8,128)} %param.41) | copy-start | bytes 24580
  1424.7 142.5 %copy-start.146 = (f32[2,64,16]{1,2,0:T(8,128)S(1)}, f32[2,64,16]{1,2,0:T(8,128)}, u32[]{:S(2)}) copy-start(f32[2,64,16]{1,2,0:T(8,128)} %param.38) | copy-start | bytes 24580
  1424.7 142.5 %copy-start.147 = (f32[2,64,16]{1,2,0:T(8,128)S(1)}, f32[2,64,16]{1,2,0:T(8,128)}, u32[]{:S(2)}) copy-start(f32[2,64,16]{1,2,0:T(8,128)} %param.37) | copy-start | bytes 24580
  (123 other events, 271.6 us)
Sparse Core Ops, SparseCore 0:
  303.4 115.5 reduce-scatter.5
  420.7 54.6 all-gather.1
  580.4 183.7 all-reduce.14
  813.6 184.1 all-reduce.12
  1091.7 184.2 all-reduce.10
  1423.2 67.6 reduce-scatter.7
  1494.4 71.8 reduce-scatter.9
where the time goes:
time: 1650 us
  waiting for transfers between devices  846 us (51%)
  local copies, waits for them, and re-layouts  291 us (18%)
  matrix products  177 us (11%)
  other arithmetic  169 us (10%)
  blocking collectives  139 us (8%)
  between operations  24.4 us (1%)
    psum x2, waiting for transfers between devices, branch_add(): total = lax.psum(partial_out, 'head')  367 us
    gather x1, local copies, waits for them, and re-layouts, per_device(): jnp.take(token_embedding_table, jnp.clip(ids_here, 0, vocab_local - 1), a...  229 us
    psum x1, waiting for transfers between devices, layer_forward(): d_one = d_sum_two + lax.psum(back_part, 'head')  173 us
    reduce_scatter x1, waiting for transfers between devices, per_device(): lax.psum_scatter(jnp.where(inside[:, None], picked.astype(jnp.float32), 0...  116 us
    unnamed x8, waiting for transfers between devices  74.1 us
    psum x1, blocking collectives, per_device(): lax.psum((sq_down, sq_up, loss_part), ('dp', 'head'))  66.1 us
    reduce_scatter x1, waiting for transfers between devices, per_device(): lax.psum_scatter(sum_up, 'dp', scatter_dimension=2, tiled=True)  64.2 us
    all_gather x1, waiting for transfers between devices, per_device(): tokens = lax.all_gather(columns, 'head', axis=1, tiled=True)  51.6 us
  transfers between devices with their start and end apart: 7, of which 7 were waited for; matrix products, arithmetic and copies ran while one was open for 1% of the time, Pallas kernels for 0%

commit v1 on v0

--- a/solution.py
+++ b/solution.py
@@ -355,7 +355,7 @@
         / n_head
     )
     sq_up = jnp.stack([jnp.sum(up_weight * up_weight, (1, 2)), jnp.sum(dir_up * dir_up, (1, 2))], 1)
-    total_down, total_up, loss_sum = lax.psum((sq_down, sq_up, loss_part), ("dp", "head"))
+    total_down, total_up, loss_sum = lax.psum(lax.psum((sq_down, sq_up, loss_part), "head"), "dp")
     norm_table = jnp.sqrt(jnp.concatenate([total_down, total_up], 0))
     updated_down = (
         down_weight - learn_rate * (norm_table[:2, 0] / norm_table[:2, 1])[:, None, None] * dir_down

time: 1650 us -> 1640 us (level)
  blocking collectives: 139 us -> 119 us
    psum x1 -> x2, blocking collectives: 66.1 us -> 46.2 us  [the longest x1 31.5 us: per_device(): lax.psum(lax.psum((sq_down, sq_up, loss_part), 'head'), 'dp')]
where the time goes in v1:
time: 1640 us; the launch traced here: 1630 us
  waiting for transfers between devices  846 us (52%)
  local copies, waits for them, and re-layouts  291 us (18%)
  matrix products  177 us (11%)
  other arithmetic  169 us (10%)
  blocking collectives  119 us (7%)
  between operations  24.4 us (1%)
    psum x2, waiting for transfers between devices, branch_add(): total = lax.psum(partial_out, 'head')  367 us
    gather x1, local copies, waits for them, and re-layouts, per_device(): jnp.take(token_embedding_table, jnp.clip(ids_here, 0, vocab_local - 1), a...  229 us
    psum x1, waiting for transfers between devices, layer_forward(): d_one = d_sum_two + lax.psum(back_part, 'head')  173 us
    reduce_scatter x1, waiting for transfers between devices, per_device(): lax.psum_scatter(jnp.where(inside[:, None], picked.astype(jnp.float32), 0...  116 us
    unnamed x8, waiting for transfers between devices  74.1 us
    reduce_scatter x1, waiting for transfers between devices, per_device(): lax.psum_scatter(sum_up, 'dp', scatter_dimension=2, tiled=True)  64.1 us
    all_gather x1, waiting for transfers between devices, per_device(): tokens = lax.all_gather(columns, 'head', axis=1, tiled=True)  51.5 us
    convert_element_type x1, other arithmetic, per_device(): jnp.where(inside[:, None], picked.astype(jnp.float32), 0.0)  46.3 us
  transfers between devices with their start and end apart: 7, of which 7 were waited for; matrix products, arithmetic and copies ran while one was open for 1% of the time, Pallas kernels for 0%

profile of v1, /device:TPU:1, one launch (start us, length us, event | category | flops | bytes accessed | tf_op | source)
XLA Modules:
  0.0 1627.0 jit_solution(5210734324515043901)
XLA Ops:
  7.3 19.8 %all_gather.9 = s32[128,512]{1,0:T(8,128)S(1)} all-gather(s32[8,512]{1,0:T(8,128)} %param.22), channel_id=1, replica_groups=mesh['dp'=16,'head'=8] {'dp'}, dimensions={0}, use_global_device_ids=true | all-gather | bytes 278528 | tf_op jit(solution)/shard_map/all_gather | solution.py:277
  28.1 228.9 %gather_fusion = bf16[65536,128]{1,0:T(8,128)(2,1)} fusion(bf16[3144,128]{1,0:T(8,128)(2,1)S(1)} %copy-done.1, s32[65536]{0:T(1024)S(1)} %broadcast_clamp_fusion), kind=kCustom, calls=%fused_computation | custom fusion | bytes 33816576 | tf_op jit(solution)/shard_map/jit(_take)/gather | solution.py:282
  257.0 46.3 %select_convert_fusion = bf16[65536,128]{1,0:T(8,128)(2,1)} fusion(bf16[65536,128]{1,0:T(8,128)(2,1)} %gather_fusion, pred[65536]{0:T(1024)(128)(4,1)S(1)} %compare_and_fusion, pred[65536]{0:T(1024)(128)(4,1)S(1)} %bitcast.555), kind=kLoop, calls=%fused_computation.1 | loop fusion | flops 33554432 | bytes 33685504 | tf_op jit(solution)/shard_map/convert_element_type | solution.py:284
  303.3 115.7 %reduce-scatter.6.cloned.1.call-done = bf16[4096,128]{1,0:T(8,128)(2,1)} async-done(((bf16[65536,128]{1,0:T(8,128)(2,1)}), bf16[4096,128]{1,0:T(8,128)(2,1)}) %reduce-scatter.6.cloned.1.call-update) | async-done | bytes 1048592 | tf_op jit(solution)/shard_map/reduce_scatter | solution.py:283
  423.8 51.5 %all-gather.2.cloned.1.call-done = bf16[4096,1024]{1,0:T(8,128)(2,1)} async-done(((bf16[4096,128]{1,0:T(8,128)(2,1)}), bf16[4096,1024]{1,0:T(8,128)(2,1)}) %all-gather.2.cloned.1.call-update) | async-done | bytes 8388624 | tf_op jit(solution)/shard_map/all_gather | solution.py:294
  475.3 5.1 fusion
  480.4 5.9 multiply_reduce_fusion
  486.4 6.1 multiply_add_fusion
  492.5 3.6 fusion.384
  496.1 4.8 fusion.383
  500.9 3.9 fusion.183
  565.8 3.3 fusion.135
  573.8 3.3 fusion.133
  580.2 183.9 %all-reduce.16.cloned.1.call-done = (f32[1024,1024]{1,0:T(8,128)}, f32[1024,1024]{1,0:T(8,128)}, f32[1024,1024]{1,0:T(8,128)}, f32[1024,1024]{1,0:T(8,128)}) async-done(((f32[1024,1024]{1,0:T(8,128)}, f32[1024,1024]{1,0:T(8,128)}, f32[1024,1024]{1,0:T(8,128)}, f32[1024,1024]{1,0:T(8,128)}), (f32[1024,1024]{1,0:T(8,128)}, f32[1024,1024]{1,0:T(8,128)}, f32[1024,1024]{1,0:T(8,128)}, ...) | async-done | bytes 16777232 | tf_op jit(solution)/shard_map/psum | solution.py:43
  764.1 4.1 fusion.382
  777.4 6.8 fusion.140
  784.3 6.7 fusion.138
  794.8 6.7 fusion.139
  806.7 6.7 fusion.137
  814.3 183.4 %all-reduce.14.cloned.1.call-done = (f32[1024,1024]{1,0:T(8,128)}, f32[1024,1024]{1,0:T(8,128)}, f32[1024,1024]{1,0:T(8,128)}, f32[1024,1024]{1,0:T(8,128)}) async-done(((f32[1024,1024]{1,0:T(8,128)}, f32[1024,1024]{1,0:T(8,128)}, f32[1024,1024]{1,0:T(8,128)}, f32[1024,1024]{1,0:T(8,128)}), (f32[1024,1024]{1,0:T(8,128)}, f32[1024,1024]{1,0:T(8,128)}, f32[1024,1024]{1,0:T(8,128)}, ...) | async-done | bytes 16777232 | tf_op jit(solution)/shard_map/psum | solution.py:43
  997.8 12.3 fusion.371
  1012.7 4.3 multiply_reduce_fusion.13
  1019.7 5.7 fusion.24
  1027.7 8.9 fusion.18
  1036.6 10.9 fusion.144
  1047.5 3.9 fusion.31
  1051.4 11.0 fusion.143
  1062.4 7.4 fusion.29
  1069.8 10.8 fusion.142
  1080.6 10.9 fusion.141
  1102.5 173.4 %all-reduce.12.cloned.1.call-done = (f32[1024,1024]{1,0:T(8,128)}, f32[1024,1024]{1,0:T(8,128)}, f32[1024,1024]{1,0:T(8,128)}, f32[1024,1024]{1,0:T(8,128)}) async-done(((f32[1024,1024]{1,0:T(8,128)}, f32[1024,1024]{1,0:T(8,128)}, f32[1024,1024]{1,0:T(8,128)}, f32[1024,1024]{1,0:T(8,128)}), (f32[1024,1024]{1,0:T(8,128)}, f32[1024,1024]{1,0:T(8,128)}, f32[1024,1024]{1,0:T(8,128)}, ...) | async-done | bytes 16777232 | tf_op jit(solution)/shard_map/psum | solution.py:146
  1275.9 7.9 fusion.370
  1286.6 3.5 convolution_convert_fusion
  1295.2 5.9 fusion.369
  1304.0 3.5 convolution_convert_fusion.1
  1307.5 3.5 multiply_reduce_fusion.4
  1312.6 5.9 fusion.368
  1321.3 3.5 convolution_convert_fusion.2
  1324.9 3.6 multiply_reduce_fusion.7
  1329.9 5.9 fusion.367
  1338.7 3.5 convolution_convert_fusion.3
  1359.7 29.7 %all-reduce.17 = (bf16[1024,32]{0,1:T(8,128)(2,1)}, bf16[1024,32]{0,1:T(8,128)(2,1)}, bf16[1024,32]{0,1:T(8,128)(2,1)}, bf16[1024,32]{0,1:T(8,128)(2,1)}) all-reduce(f32[1024,32]{0,1:T(8,128)S(1)} %maximum_multiply_fusion.3, f32[1024,32]{0,1:T(8,128)} %maximum_multiply_fusion.2, ...), channel_id=1, replica_groups=mesh['dp'=16,'head'=8] {'head'}, use_global_device_ids=true, to_apply=%region_74.76 | all-reduce | flops 131072 | bytes 786432 | tf_op jit(solution)/shard_map/psum | solution.py:201
  1396.7 10.8 all_to_all.6
  1409.6 12.5 all-reduce
  1426.7 64.1 %reduce-scatter.8.cloned.1.call-done = f32[2,16,8]{1,2,0:T(8,128)} async-done(((f32[2,16,128]{1,2,0:T(8,128)}), f32[2,16,8]{1,2,0:T(8,128)}) %reduce-scatter.8.cloned.1.call-update) | async-done | bytes 1040 | tf_op jit(solution)/shard_map/reduce_scatter | solution.py:331
  1492.2 74.0 %reduce-scatter.10.cloned.1.call-done = f32[64,32]{1,0:T(8,128)} async-done(((f32[1024,32]{1,0:T(8,128)}), f32[64,32]{1,0:T(8,128)}) %reduce-scatter.10.cloned.1.call-update) | async-done | bytes 8208
  1568.6 14.7 all-reduce.2
  1583.3 31.5 %all-reduce.1 = (f32[]{:T(128)}, f32[2,2]{0,1:T(2,128)S(1)}, f32[2,2]{0,1:T(2,128)S(1)}) all-reduce(f32[]{:T(128)} %get-tuple-element.32, f32[2,2]{0,1:T(2,128)S(1)} %get-tuple-element.33, f32[2,2]{0,1:T(2,128)S(1)} %get-tuple-element.34), channel_id=1, replica_groups=mesh['dp'=16,'head'=8] {'dp'}, use_global_device_ids=true, to_apply=%region_46.48 | all-reduce | flops 9 | bytes 72 | tf_op jit(solution)/shard_map/psum | solution.py:358
  (612 shorter events, 162.8 us)
Async XLA Ops:
  7.2 770.2 %copy-start = (bf16[512,1024]{1,0:T(8,128)(2,1)S(1)}, bf16[512,1024]{1,0:T(8,128)(2,1)}, u32[]{:S(2)}) copy-start(bf16[512,1024]{1,0:T(8,128)(2,1)} %param.31) | copy-start | bytes 3145732
  7.2 20.9 %copy-start.1 = (bf16[3144,128]{1,0:T(8,128)(2,1)S(1)}, bf16[3144,128]{1,0:T(8,128)(2,1)}, u32[]{:S(2)}) copy-start(bf16[3144,128]{1,0:T(8,128)(2,1)} %param.26) | copy-start | bytes 2414596
  7.2 411.9 %reduce-scatter.6.cloned.1.call-start = ((), (), s32[]{:S(2)}) async-start(), calls=%async_computation.4 | async-start | bytes 17825792 | tf_op jit(solution)/shard_map/reduce_scatter | solution.py:283
  303.3 172.0 %all-gather.2.cloned.1.call-start = ((), (), s32[]{:S(2)}) async-start(), calls=%async_computation.5 | async-start | bytes 9437184 | tf_op jit(solution)/shard_map/all_gather | solution.py:294
  419.1 345.0 %all-reduce.16.cloned.1.call-start = ((), (), s32[]{:S(2)}) async-start(), calls=%async_computation.10 | async-start | bytes 33554432 | tf_op jit(solution)/shard_map/psum | solution.py:43
  420.7 151.5 %copy-start.88 = (bf16[2,16,128]{2,1,0:T(8,128)(2,1)}, bf16[2,16,128]{2,1,0:T(8,128)(2,1)S(1)}, u32[]{:S(2)}) copy-start(bf16[2,16,128]{2,1,0:T(8,128)(2,1)S(1)} %convert_element_type.351) | copy-start | bytes 24580
  422.0 151.2 %copy-start.111 = (pred[2,512]{1,0:T(4,128)(4,1)}, pred[2,512]{1,0:T(4,128)(4,1)S(1)}, u32[]{:S(2)}) copy-start(pred[2,512]{1,0:T(4,128)(4,1)S(1)} %get-tuple-element.140) | copy-start | bytes 3076
  500.9 19.8 %copy-start.32 = (f32[2,512,1024]{2,1,0:T(8,128)}, f32[2,512,1024]{2,1,0:T(8,128)S(1)}, u32[]{:S(2)}) copy-start(f32[2,512,1024]{2,1,0:T(8,128)S(1)} %get-tuple-element.82) | copy-start | bytes 12582916
  523.1 14.8 copy-start.71
  524.8 8.6 copy-start.53
  527.1 7.3 copy-start.49
  542.6 15.3 copy-start.69
  544.3 9.1 copy-start.55
  547.2 7.3 copy-start.51
  580.2 417.6 %all-reduce.14.cloned.1.call-start = ((), (), s32[]{:S(2)}) async-start(), calls=%async_computation.9 | async-start | bytes 33554432 | tf_op jit(solution)/shard_map/psum | solution.py:43
  764.1 4.7 copy-start.48
  768.2 5.0 copy-start.26
  777.4 6.8 copy-start.160
  784.3 6.7 copy-start.29
  784.3 6.7 copy-start.47
  794.8 6.7 copy-start.163
  794.8 6.7 copy-start.28
  794.8 6.7 copy-start.46
  813.4 462.5 %all-reduce.12.cloned.1.call-start = ((), (), s32[]{:S(2)}) async-start(), calls=%async_computation.8 | async-start | bytes 33554432 | tf_op jit(solution)/shard_map/psum | solution.py:146
  1010.0 9.6 copy-start.2
  1010.0 9.6 copy-start.6
  1010.0 17.6 %copy-start.4 = (f32[1024,1024]{1,0:T(8,128)}, f32[1024,1024]{1,0:T(8,128)S(1)}, u32[]{:S(2)}) copy-start(f32[1024,1024]{1,0:T(8,128)S(1)} %get-tuple-element.124) | copy-start | bytes 12582916
  1010.1 17.6 %copy-start.8 = (f32[1024,1024]{1,0:T(8,128)}, f32[1024,1024]{1,0:T(8,128)S(1)}, u32[]{:S(2)}) copy-start(f32[1024,1024]{1,0:T(8,128)S(1)} %get-tuple-element.128) | copy-start | bytes 12582916
  1012.7 4.3 copy-start.158
  1091.6 399.3 %reduce-scatter.8.cloned.1.call-start = ((), (), s32[]{:S(2)}) async-start(), calls=%async_computation.6 | async-start | bytes 139264 | tf_op jit(solution)/shard_map/reduce_scatter | solution.py:331
  1275.9 7.9 copy-start.27
  1275.9 7.9 copy-start.45
  1290.2 53.7 %copy-start.78 = (bf16[2,2,64,512]{3,2,1,0:T(8,128)(2,1)}, bf16[2,2,64,512]{3,2,1,0:T(8,128)(2,1)S(1)}, u32[]{:S(2)}) copy-start(bf16[2,2,64,512]{3,2,1,0:T(8,128)(2,1)S(1)} %convolution_convert_fusion) | copy-start | bytes 786436
  1290.2 5.0 copy-start.25
  1307.5 40.5 %copy-start.80 = (bf16[2,2,64,512]{3,2,1,0:T(8,128)(2,1)}, bf16[2,2,64,512]{3,2,1,0:T(8,128)(2,1)S(1)}, u32[]{:S(2)}) copy-start(bf16[2,2,64,512]{3,2,1,0:T(8,128)(2,1)S(1)} %convolution_convert_fusion.1) | copy-start | bytes 786436
  1307.5 5.1 copy-start.23
  1324.8 27.4 %copy-start.82 = (bf16[2,2,64,512]{3,2,1,0:T(8,128)(2,1)}, bf16[2,2,64,512]{3,2,1,0:T(8,128)(2,1)S(1)}, u32[]{:S(2)}) copy-start(bf16[2,2,64,512]{3,2,1,0:T(8,128)(2,1)S(1)} %convolution_convert_fusion.2) | copy-start | bytes 786436
  1324.9 5.1 copy-start.21
  1342.2 13.8 copy-start.84
  1358.9 32.7 %copy-start.38 = (bf16[2,512,1024]{2,1,0:T(8,128)(2,1)S(1)}, bf16[2,512,1024]{2,1,0:T(8,128)(2,1)}, u32[]{:S(2)}) copy-start(bf16[2,512,1024]{2,1,0:T(8,128)(2,1)} %get-tuple-element.87) | copy-start | bytes 6291460
  1423.1 143.1 %reduce-scatter.10.cloned.1.call-start = ((), (), s32[]{:S(2)}) async-start(), calls=%async_computation.7 | async-start | bytes 557056
  1423.2 67.7 %copy-start.122 = (f32[2,16,8]{1,2,0:T(8,128)S(1)}, f32[2,16,8]{1,2,0:T(8,128)}, u32[]{:S(2)}) copy-start(f32[2,16,8]{1,2,0:T(8,128)} %copy.338) | copy-start | bytes 3076
  1423.2 67.7 %copy-start.153 = (f32[2,16,8]{1,2,0:T(8,128)S(1)}, f32[2,16,8]{1,2,0:T(8,128)}, u32[]{:S(2)}) copy-start(f32[2,16,8]{1,2,0:T(8,128)} %param.42) | copy-start | bytes 3076
  1423.2 67.7 %copy-start.154 = (f32[2,16,8]{1,2,0:T(8,128)S(1)}, f32[2,16,8]{1,2,0:T(8,128)}, u32[]{:S(2)}) copy-start(f32[2,16,8]{1,2,0:T(8,128)} %param.40) | copy-start | bytes 3076
  1423.2 67.7 %copy-start.155 = (f32[2,16,8]{1,2,0:T(8,128)S(1)}, f32[2,16,8]{1,2,0:T(8,128)}, u32[]{:S(2)}) copy-start(f32[2,16,8]{1,2,0:T(8,128)} %param.39) | copy-start | bytes 3076
  1424.7 142.5 %copy-start.145 = (f32[2,64,16]{1,2,0:T(8,128)S(1)}, f32[2,64,16]{1,2,0:T(8,128)}, u32[]{:S(2)}) copy-start(f32[2,64,16]{1,2,0:T(8,128)} %param.41) | copy-start | bytes 24580
  1424.7 142.5 %copy-start.146 = (f32[2,64,16]{1,2,0:T(8,128)S(1)}, f32[2,64,16]{1,2,0:T(8,128)}, u32[]{:S(2)}) copy-start(f32[2,64,16]{1,2,0:T(8,128)} %param.38) | copy-start | bytes 24580
  1424.7 142.5 %copy-start.147 = (f32[2,64,16]{1,2,0:T(8,128)S(1)}, f32[2,64,16]{1,2,0:T(8,128)}, u32[]{:S(2)}) copy-start(f32[2,64,16]{1,2,0:T(8,128)} %param.37) | copy-start | bytes 24580
  (123 other events, 271.6 us)
Sparse Core Ops, SparseCore 0:
  303.4 115.6 reduce-scatter.5
  420.7 54.5 all-gather.1
  580.3 183.7 all-reduce.15
  813.5 184.1 all-reduce.13
  1091.7 184.1 all-reduce.11
  1423.2 67.5 reduce-scatter.7
  1494.4 71.8 reduce-scatter.9
